TPU v7x, 32 devices: a whole 2x2x4 slice. The times are simulated.
32 devices in a mesh: row: 4 (over y, x), col: 8 (over z, core).
Axes of the slice: x: 2, y: 2, z: 4, core: 2. Of those that a mesh axis runs over, the one named last changes fastest.
Arguments:
- stiffness: float32 [12, 4, 128, 6144], P(None, 'row', None, 'col'), may hold values from -8 to 8
- lower_first: float32 [1024, 10, 4, 128], P('col', None, 'row'), may hold values from -0.1875 to 0.1875
- lower_second: float32 [1024, 8, 4, 128], P('col', None, 'row'), may hold values from -0.1875 to 0.1875
- diag_inv: float32 [2, 1024, 2, 4, 128], P(None, 'col', None, 'row'), as said below
Outputs:
- reduced: float32 [12, 4, 128, 6144], P(None, 'row', None, 'col')
Inputs may be any that keep to these rules, and one draw needn't show every extreme that they name: Each block of diag_inv, read as a 1024 x 1024 matrix, is zero above its diagonal and has a positive diagonal.
All inputs are finite; a program needn't handle non-finite values.
Results may differ from a plain program's by a relative error of at most 0.000086.
Values sent between devices are 32-bit elements; how exact they have to be, the bound alone decides.
A program may use at most 128 MiB of HBM per device.

v0:
```python
import jax
import jax.numpy as jnp
from jax import lax
from jax.sharding import PartitionSpec as P


def product(left, right):
    return jnp.dot(left, right, precision=lax.Precision.HIGH, preferred_element_type=jnp.float32)


def apply_cols(columns, factor):
    return lax.dot_general(
        columns,
        factor,
        (((0,), (0,)), ((), ())),
        precision=lax.Precision.HIGH,
        preferred_element_type=jnp.float32,
    )


def shards(stiffness, lower_first, lower_second, diag_inv):
    cycles = stiffness.shape[0]
    rblk = stiffness.shape[2]
    cdev = stiffness.shape[3]
    pcount = diag_inv.shape[2]
    nrow = lax.axis_size("row")
    nb = diag_inv.shape[1] * lax.axis_size("col")
    height = pcount * rblk
    matrix_rows = stiffness.reshape(cycles * rblk, cdev)
    inv_cols = lax.all_gather(diag_inv, "col", axis=1, tiled=True)
    inverse = inv_cols.reshape(2, nb, height)

    def own_rows(solved):
        grouped = solved.reshape(pcount, nrow, rblk, cdev)
        mine = lax.dynamic_slice_in_dim(grouped, lax.axis_index("row"), 1, 1)
        return mine.reshape(height, cdev)

    w_first = lax.psum(product(inverse[0], matrix_rows[:height]), "row")
    coupling = lax.all_gather(lower_first[:, :pcount], "col", axis=0, tiled=True).reshape(
        nb, height
    )
    w_second = lax.psum(
        product(inverse[1], matrix_rows[height : 2 * height] - apply_cols(coupling, w_first)), "row"
    )
    pieces = (
        lax.all_gather(lower_first[:, pcount:], "col", axis=0, tiled=True),
        lax.all_gather(lower_second, "col", axis=0, tiled=True),
    )
    count = pieces[0].shape[0]
    first_piece = pieces[0].reshape(count, -1)
    second_piece = pieces[1].reshape(count, -1)
    remain = (
        matrix_rows[2 * height :]
        - apply_cols(first_piece, w_first)
        - apply_cols(second_piece, w_second)
    )
    stacked = jnp.concatenate([own_rows(w_first), own_rows(w_second), remain], axis=0)
    return stacked.reshape(cycles, 1, rblk, cdev)


def solution(mesh):
    placed = (
        P(None, "row", None, "col"),
        P("col", None, "row", None),
        P("col", None, "row", None),
        P(None, "col", None, "row", None),
    )
    return jax.shard_map(
        shards, mesh=mesh, in_specs=placed, out_specs=P(None, "row", None, "col"), check_vma=False
    )
```

profile of v0, /device:TPU:0, one launch (start us, length us, event | category | flops | bytes accessed | tf_op | source)
XLA Modules:
  0.0 369.2 jit_solution(9611690720741950493)
XLA Ops:
  6.5 0.0 all-gather.5.cloned.1.call-start
  6.5 0.7 all-gather.5.cloned.1.call-update
  7.3 0.0 all-gather.7.cloned.1.call-start
  7.3 1.6 slice.37
  8.9 0.0 all-gather.7.cloned.1.call-update
  8.9 0.0 all-reduce.3.cloned.1.call-start
  8.9 1.5 fusion.16
  10.4 30.4 %all-gather.5.cloned.1.call-done = f32[2,1024,2,1,128]{4,3,2,1,0:T(1,128)} async-done(((f32[2,128,2,1,128]{4,3,2,1,0:T(1,128)}), f32[2,1024,2,1,128]{4,3,2,1,0:T(1,128)}) %all-gather.5.cloned.1.call-update) | async-done | bytes 2097168 | tf_op jit(solution)/shard_map/all_gather | solution.py:30
  40.8 7.8 %slice_reduce_fusion = (f32[1024,2,128]{2,1,0:T(2,128)S(1)}, f32[1024,2,128]{2,1,0:T(2,128)S(1)}) fusion(f32[2,1024,2,1,128]{4,3,2,1,0:T(1,128)} %all-gather.5.cloned.1.call-done), kind=kLoop, calls=%fused_computation.19 | loop fusion | bytes 4194304 | tf_op jit(solution)/shard_map/slice | solution.py:43
  48.7 3.1 fusion.13
  51.8 0.0 all-reduce.3.cloned.1.call-update
  51.8 0.0 all-reduce.5.cloned.1.call-start
  51.9 0.3 copy.21
  52.2 12.0 %all-gather.7.cloned.1.call-done = f32[1024,2,1,128]{3,1,2,0:T(2,128)} async-done(((f32[128,2,1,128]{3,1,2,0:T(2,128)}), f32[1024,2,1,128]{3,1,2,0:T(2,128)}) %all-gather.7.cloned.1.call-update) | async-done | bytes 1048592 | tf_op jit(solution)/shard_map/all_gather | solution.py:39
  64.1 89.7 %all-reduce.3.cloned.1.call-done = f32[1024,768]{1,0:T(8,128)} async-done(((f32[1024,768]{1,0:T(8,128)}), f32[1024,768]{1,0:T(8,128)}) %all-reduce.3.cloned.1.call-update) | async-done | bytes 3145744 | tf_op jit(solution)/shard_map/psum | solution.py:38
  153.8 4.8 %fusion.8 = f32[256,768]{0,1:T(8,128)S(1)} fusion(f32[256,768]{0,1:T(8,128)S(1)} %copy.21, f32[1024,768]{1,0:T(8,128)} %all-reduce.3.cloned.1.call-done, f32[128,8,2,128]{3,2,1,0:T(2,128)} %bitcast.76), kind=kOutput, calls=%fused_computation.11 | convolution fusion | flops 1208156160 | bytes 5767168 | tf_op jit(solution)/shard_map/dot_general | solution.py:12
  158.6 0.0 copy-start.3
  158.6 3.1 convolution_bitcast_fusion
  161.7 0.0 all-reduce.5.cloned.1.call-update
  161.7 0.0 all-gather.11.cloned.1.call-start
  161.8 0.5 all-gather.11.cloned.1.call-update
  162.3 0.2 all-gather.9.cloned.1.call-start
  162.5 0.0 copy-done.3
  162.6 0.8 slice.41
  163.4 0.0 all-gather.9.cloned.1.call-update
  163.4 3.8 %slice.39 = f32[8,1,128,768]{3,2,1,0:T(8,128)} slice(f32[12,1,128,768]{3,2,1,0:T(8,128)} %param.4), slice={[4:12], [0:1], [0:128], [0:768]} | slice | bytes 6291456 | tf_op jit(solution)/shard_map/slice | solution.py:53
  167.2 0.0 copy-start
  167.2 4.1 %copy.22 = f32[1024,768]{0,1:T(8,128)} copy(f32[1024,768]{1,0:T(8,128)} %bitcast.65) | data formatting | bytes 6291456 | tf_op jit(solution)/shard_map/slice | solution.py:53
  171.3 0.0 copy-done
  171.3 0.9 constant_dynamic-slice_fusion
  172.3 2.3 copy.20
  174.6 74.3 %all-reduce.5.cloned.1.call-done = f32[1024,768]{0,1:T(8,128)} async-done(((f32[1024,768]{0,1:T(8,128)}), f32[1024,768]{0,1:T(8,128)}) %all-reduce.5.cloned.1.call-update) | async-done | bytes 3145744 | tf_op jit(solution)/shard_map/psum | solution.py:42
  248.8 5.1 %reshape.36 = f32[2,4,128,768]{2,1,0,3:T(4,128)} reshape(f32[1024,768]{0,1:T(8,128)} %all-reduce.5.cloned.1.call-done) | data formatting | bytes 6291456 | tf_op jit(solution)/shard_map/reshape | solution.py:34
  254.0 4.6 %dynamic-slice_reduce_fusion = f32[2,128,768]{1,0,2:T(2,128)S(1)} fusion(f32[2,4,128,768]{2,1,0,3:T(4,128)} %reshape.36, s32[]{:T(128)S(6)} %select_n.4), kind=kLoop, calls=%fused_computation.22 | loop fusion | bytes 1572868 | tf_op jit(solution)/shard_map/dynamic_slice | solution.py:35
  258.5 0.9 copy.54
  259.5 37.7 %all-gather.11.cloned.1.call-done = f32[1024,8,1,128]{3,1,2,0:T(8,128)} async-done(((f32[128,8,1,128]{3,1,2,0:T(8,128)}), f32[1024,8,1,128]{3,1,2,0:T(8,128)}) %all-gather.11.cloned.1.call-update) | async-done | bytes 4194320 | tf_op jit(solution)/shard_map/all_gather | solution.py:47
  297.2 9.6 %fusion = f32[768,1024]{1,0:T(8,128)} fusion(f32[1024,768]{0,1:T(8,128)} %all-reduce.5.cloned.1.call-done, f32[128,8,8,128]{3,2,1,0:T(8,128)} %bitcast.66), kind=kOutput, calls=%fused_computation.1 | convolution fusion | flops 4831838208 | bytes 10485760 | tf_op jit(solution)/shard_map/dot_general | solution.py:12
  306.8 37.6 %all-gather.9.cloned.1.call-done = f32[1024,8,1,128]{3,1,2,0:T(8,128)} async-done(((f32[128,8,1,128]{3,1,2,0:T(8,128)}), f32[1024,8,1,128]{3,1,2,0:T(8,128)}) %all-gather.9.cloned.1.call-update) | async-done | bytes 4194320 | tf_op jit(solution)/shard_map/all_gather | solution.py:46
  344.3 0.0 copy-start.1
  344.3 0.0 copy-start.2
  344.3 9.4 %bitcast_subtract_fusion = f32[1024,768]{0,1:T(8,128)S(1)} fusion(f32[768,1024]{1,0:T(8,128)} %fusion, f32[1024,768]{0,1:T(8,128)} %copy.22, f32[1024,768]{1,0:T(8,128)S(1)} %copy-done, f32[128,8,8,128]{3,2,1,0:T(8,128)} %bitcast.69), kind=kOutput, calls=%fused_computation.7 | convolution fusion | flops 4833411072 | bytes 16777216 | tf_op jit(solution)/shard_map/dot_general | solution.py:12
  353.7 0.0 copy-done.1
  353.8 0.0 copy-done.2
  353.8 2.6 pad_maximum_fusion
  356.4 6.0 %copy.18 = f32[1536,768]{1,0:T(8,128)} copy(f32[1536,768]{0,1:T(8,128)} %pad_maximum_fusion) | data formatting | bytes 9437184 | tf_op jit(solution)/shard_map/concatenate | solution.py:57
Async XLA Ops:
  6.5 34.3 %all-gather.5.cloned.1.call-start = ((), (), s32[]{:S(2)}) async-start(), calls=%async_computation | async-start | bytes 2359296 | tf_op jit(solution)/shard_map/all_gather | solution.py:30
  7.3 56.9 %all-gather.7.cloned.1.call-start = ((), (), s32[]{:S(2)}) async-start(), calls=%async_computation.2 | async-start | bytes 1179648 | tf_op jit(solution)/shard_map/all_gather | solution.py:39
  8.9 144.9 %all-reduce.3.cloned.1.call-start = ((), (), s32[]{:S(2)}) async-start(), calls=%async_computation.1 | async-start | bytes 6291456 | tf_op jit(solution)/shard_map/psum | solution.py:38
  51.8 197.0 %all-reduce.5.cloned.1.call-start = ((), (), s32[]{:S(2)}) async-start(), calls=%async_computation.3 | async-start | bytes 6291456 | tf_op jit(solution)/shard_map/psum | solution.py:42
  158.6 4.0 %copy-start.3 = (f32[128,10,1,128]{3,2,1,0:T(1,128)S(1)}, f32[128,10,1,128]{3,2,1,0:T(1,128)}, u32[]{:S(2)}) copy-start(f32[128,10,1,128]{3,2,1,0:T(1,128)} %param.5) | copy-start | bytes 1966084
  161.7 135.4 %all-gather.11.cloned.1.call-start = ((), (), s32[]{:S(2)}) async-start(), calls=%async_computation.5 | async-start | bytes 4718592 | tf_op jit(solution)/shard_map/all_gather | solution.py:47
  162.3 182.0 %all-gather.9.cloned.1.call-start = ((), (), s32[]{:S(2)}) async-start(), calls=%async_computation.4 | async-start | bytes 4718592 | tf_op jit(solution)/shard_map/all_gather | solution.py:46
  167.2 4.1 %copy-start = (f32[1024,768]{1,0:T(8,128)S(1)}, f32[1024,768]{1,0:T(8,128)}, u32[]{:S(2)}) copy-start(f32[1024,768]{1,0:T(8,128)} %all-reduce.3.cloned.1.call-done) | copy-start | bytes 9437188
  344.3 9.4 %copy-start.1 = (f32[256,768]{0,1:T(8,128)S(1)}, f32[256,768]{0,1:T(8,128)}, u32[]{:S(2)}) copy-start(f32[256,768]{0,1:T(8,128)} %copy.20) | copy-start | bytes 2359300
  344.3 9.4 %copy-start.2 = (f32[96,8,2,128]{3,1,2,0:T(8,128)S(1)}, f32[96,8,2,128]{3,1,2,0:T(8,128)}, u32[]{:S(2)}) copy-start(f32[96,8,2,128]{3,1,2,0:T(8,128)} %copy.54) | copy-start | bytes 2359300
Sparse Core Ops, SparseCore 0:
  8.9 31.8 all-gather.4
  42.4 21.6 all-gather.6
  67.2 86.5 all-reduce.2
  161.9 86.9 all-reduce.4
  250.3 46.8 all-gather.10
  298.6 45.6 all-gather.8
where the time goes:
time: 370 us; the launch traced here: 369 us
  waiting for transfers between devices  283 us (76%)
  local copies, waits for them, and re-layouts  39.8 us (11%)
  matrix products  30 us (8%)
  between operations  13.6 us (4%)
    psum x1, waiting for transfers between devices, shards(): w_first = lax.psum(product(inverse[0], matrix_rows[:height]), 'row')  89.7 us
    psum x1, waiting for transfers between devices, shards(): lax.psum(product(inverse[1], matrix_rows[height:2 * height] - apply_cols(...  74.3 us
    all_gather x1, waiting for transfers between devices, shards(): lax.all_gather(lower_second, 'col', axis=0, tiled=True)  37.7 us
    all_gather x1, waiting for transfers between devices, shards(): lax.all_gather(lower_first[:, pcount:], 'col', axis=0, tiled=True)  37.6 us
    all_gather x1, waiting for transfers between devices, shards(): inv_cols = lax.all_gather(diag_inv, 'col', axis=1, tiled=True)  30.4 us
    dot_general x3, matrix products, apply_cols(): lax.dot_general(columns, factor, (((0,), (0,)), ((), ())), precision=lax....  23.8 us
    all_gather x1, waiting for transfers between devices, shards(): lax.all_gather(lower_first[:, :pcount], 'col', axis=0, tiled=True)  12 us
    slice x2, local copies, waits for them, and re-layouts, shards(): matrix_rows[2 * height:] - apply_cols(first_piece, w_first)  7.89 us
  transfers between devices with their start and end apart: 6, of which 6 were waited for; matrix products, arithmetic and copies ran while one was open for 13% of the time, Pallas kernels for 0%

commit v1 on v0

--- a/solution.py
+++ b/solution.py
@@ -2,6 +2,16 @@
 import jax.numpy as jnp
 from jax import lax
 from jax.sharding import PartitionSpec as P
+
+
+def around_the_ring(block, axis, dim):
+    devices = lax.axis_size(axis)
+    held, blocks = (block, [block])
+    for _ in range(devices - 1):
+        held = lax.ppermute(held, axis, [(i, (i + 1) % devices) for i in range(devices)])
+        blocks.insert(0, held)
+    line = jnp.concatenate(blocks, axis=dim)
+    return jnp.roll(line, (lax.axis_index(axis) + 1) * block.shape[dim], axis=dim)
 
 
 def product(left, right):
@@ -27,7 +37,7 @@
     nb = diag_inv.shape[1] * lax.axis_size("col")
     height = pcount * rblk
     matrix_rows = stiffness.reshape(cycles * rblk, cdev)
-    inv_cols = lax.all_gather(diag_inv, "col", axis=1, tiled=True)
+    inv_cols = around_the_ring(diag_inv, "col", 1)
     inverse = inv_cols.reshape(2, nb, height)
 
     def own_rows(solved):

time: 370 us -> 295 us (0.80)
  waiting for transfers between devices: 283 us -> 211 us
  local copies, waits for them, and re-layouts: 39.8 us -> 35.6 us
    ppermute x0 -> x7, waiting for transfers between devices: none -> 50.9 us  [around_the_ring(): lax.ppermute(held, axis, [(i, (i + 1) % devices) for i in range(devices)])]
    all_gather x1, waiting for transfers between devices: 37.7 us -> 0.01 us  [shards(): lax.all_gather(lower_second, 'col', axis=0, tiled=True)]
    all_gather x1, waiting for transfers between devices: 37.6 us -> 0.01 us  [shards(): lax.all_gather(lower_first[:, pcount:], 'col', axis=0, tiled=True)]
    all_gather x1 -> x0, waiting for transfers between devices: 30.4 us -> none  [shards(): inv_cols = lax.all_gather(diag_inv, 'col', axis=1, tiled=True)]
    all_gather x1, waiting for transfers between devices: 12 us -> 0.02 us  [shards(): lax.all_gather(lower_first[:, :pcount], 'col', axis=0, tiled=True)]
    reshape x1 -> x0, local copies, waits for them, and re-layouts: 5.13 us -> none  [own_rows(): grouped = solved.reshape(pcount, nrow, rblk, cdev)]
    psum x1, waiting for transfers between devices: 89.7 us -> 85.3 us  [shards(): w_first = lax.psum(product(inverse[0], matrix_rows[:height]), 'row')]
  transfers between devices with their start and end apart: 6 -> 12, of which waited for: 6 -> 9; matrix products, arithmetic and copies ran while one was open for 13% -> 14% of each run, Pallas kernels for 0% -> 0%
where the time goes in v1:
time: 295 us
  waiting for transfers between devices  211 us (72%)
  local copies, waits for them, and re-layouts  35.6 us (12%)
  matrix products  30.2 us (10%)
  between operations  14.8 us (5%)
    psum x1, waiting for transfers between devices, shards(): w_first = lax.psum(product(inverse[0], matrix_rows[:height]), 'row')  85.3 us
    psum x1, waiting for transfers between devices, shards(): lax.psum(product(inverse[1], matrix_rows[height:2 * height] - apply_cols(...  73.9 us
    ppermute x7, waiting for transfers between devices, around_the_ring(): lax.ppermute(held, axis, [(i, (i + 1) % devices) for i in range(devices)])  50.9 us
    dot_general x3, matrix products, apply_cols(): lax.dot_general(columns, factor, (((0,), (0,)), ((), ())), precision=lax....  23.9 us
    slice x2, local copies, waits for them, and re-layouts, shards(): matrix_rows[2 * height:] - apply_cols(first_piece, w_first)  7.89 us
    slice x1, local copies, waits for them, and re-layouts, shards(): inverse[1]  6.61 us
    dot_general x2, matrix products, product(): jnp.dot(left, right, precision=lax.Precision.HIGH, preferred_element_type...  6.25 us
    concatenate x1, local copies, waits for them, and re-layouts, shards(): jnp.concatenate([own_rows(w_first), own_rows(w_second), remain], axis=0)  6.04 us
  transfers between devices with their start and end apart: 12, of which 9 were waited for; matrix products, arithmetic and copies ran while one was open for 14% of the time, Pallas kernels for 0%

profile of v1, /device:TPU:0, one launch (start us, length us, event | category | flops | bytes accessed | tf_op | source)
XLA Modules:
  0.0 294.9 jit_solution(480246162438617097)
XLA Ops:
  7.4 0.0 all-gather.4.cloned.1.call-start
  7.4 0.5 collective-permute-start
  7.9 8.4 %collective-permute-done = f32[2,128,2,1,128]{4,3,2,1,0:T(1,128)S(1)} collective-permute-done((f32[2,128,2,1,128]{4,3,2,1,0:T(1,128)}, f32[2,128,2,1,128]{4,3,2,1,0:T(1,128)S(1)}, u32[]{:S(2)}, u32[]{:S(2)}) %collective-permute-start) | collective-permute-done | bytes 262176 | tf_op jit(solution)/shard_map/ppermute | solution.py:11
  16.2 0.0 collective-permute-start.1
  16.2 7.6 %collective-permute-done.1 = f32[2,128,2,1,128]{4,3,2,1,0:T(1,128)S(1)} collective-permute-done((f32[2,128,2,1,128]{4,3,2,1,0:T(1,128)S(1)}, f32[2,128,2,1,128]{4,3,2,1,0:T(1,128)S(1)}, u32[]{:S(2)}, u32[]{:S(2)}) %collective-permute-start.1) | collective-permute-done | bytes 262176 | tf_op jit(solution)/shard_map/ppermute | solution.py:11
  23.8 0.0 collective-permute-start.2
  23.8 7.6 %collective-permute-done.2 = f32[2,128,2,1,128]{4,3,2,1,0:T(1,128)S(1)} collective-permute-done((f32[2,128,2,1,128]{4,3,2,1,0:T(1,128)S(1)}, f32[2,128,2,1,128]{4,3,2,1,0:T(1,128)S(1)}, u32[]{:S(2)}, u32[]{:S(2)}) %collective-permute-start.2) | collective-permute-done | bytes 262176 | tf_op jit(solution)/shard_map/ppermute | solution.py:11
  31.4 0.0 collective-permute-start.3
  31.4 7.6 %collective-permute-done.3 = f32[2,128,2,1,128]{4,3,2,1,0:T(1,128)S(1)} collective-permute-done((f32[2,128,2,1,128]{4,3,2,1,0:T(1,128)S(1)}, f32[2,128,2,1,128]{4,3,2,1,0:T(1,128)S(1)}, u32[]{:S(2)}, u32[]{:S(2)}) %collective-permute-start.3) | collective-permute-done | bytes 262176 | tf_op jit(solution)/shard_map/ppermute | solution.py:11
  39.0 0.0 collective-permute-start.4
  39.0 7.6 %collective-permute-done.4 = f32[2,128,2,1,128]{4,3,2,1,0:T(1,128)S(1)} collective-permute-done((f32[2,128,2,1,128]{4,3,2,1,0:T(1,128)S(1)}, f32[2,128,2,1,128]{4,3,2,1,0:T(1,128)S(1)}, u32[]{:S(2)}, u32[]{:S(2)}) %collective-permute-start.4) | collective-permute-done | bytes 262176 | tf_op jit(solution)/shard_map/ppermute | solution.py:11
  46.6 0.0 collective-permute-start.5
  46.6 1.6 slice.38
  48.2 0.0 all-gather.4.cloned.1.call-update
  48.2 0.0 all-reduce.3.cloned.1.call-start
  48.3 5.9 %collective-permute-done.5 = f32[2,128,2,1,128]{4,3,2,1,0:T(1,128)S(1)} collective-permute-done((f32[2,128,2,1,128]{4,3,2,1,0:T(1,128)S(1)}, f32[2,128,2,1,128]{4,3,2,1,0:T(1,128)S(1)}, u32[]{:S(2)}, u32[]{:S(2)}) %collective-permute-start.5) | collective-permute-done | bytes 262176 | tf_op jit(solution)/shard_map/ppermute | solution.py:11
  54.2 0.0 collective-permute-start.6
  54.2 1.5 fusion.17
  55.7 6.3 %collective-permute-done.6 = f32[2,128,2,1,128]{4,3,2,1,0:T(1,128)S(1)} collective-permute-done((f32[2,128,2,1,128]{4,3,2,1,0:T(1,128)S(1)}, f32[2,128,2,1,128]{4,3,2,1,0:T(1,128)S(1)}, u32[]{:S(2)}, u32[]{:S(2)}) %collective-permute-start.6) | collective-permute-done | bytes 262176 | tf_op jit(solution)/shard_map/ppermute | solution.py:11
  62.0 0.2 constant_dynamic-update-slice_fusion.15
  62.2 0.2 constant_dynamic-update-slice_fusion.14
  62.4 0.2 constant_dynamic-update-slice_fusion.13
  62.6 0.2 constant_dynamic-update-slice_fusion.12
  62.8 0.2 constant_dynamic-update-slice_fusion.11
  63.0 0.2 constant_dynamic-update-slice_fusion.10
  63.2 0.2 constant_dynamic-update-slice_fusion.9
  63.4 0.0 copy-done.3
  63.4 0.2 constant_dynamic-update-slice_fusion.8
  63.6 0.2 constant_dynamic-update-slice_fusion.7
  63.8 0.2 constant_dynamic-update-slice_fusion.6
  64.0 0.2 constant_dynamic-update-slice_fusion.5
  64.2 0.2 constant_dynamic-update-slice_fusion.4
  64.4 0.2 constant_dynamic-update-slice_fusion.3
  64.6 0.2 constant_dynamic-update-slice_fusion.2
  64.9 0.2 constant_dynamic-update-slice_fusion.1
  65.1 0.2 constant_dynamic-update-slice_fusion
  65.3 6.6 %dynamic-slice_reduce_fusion = (f32[1024,2,128]{2,1,0:T(2,128)S(1)}, f32[1024,2,128]{2,1,0:T(2,128)S(1)}) fusion(f32[2,2048,2,1,128]{4,3,2,1,0:T(1,128)S(1)} %constant_dynamic-update-slice_fusion, s32[]{:T(128)S(6)} %add.29, s32[]{:T(128)S(6)} %select_n.18), kind=kLoop, calls=%fused_computation.19 | loop fusion | bytes 4194312 | tf_op jit(solution)/shard_map/slice | solution.py:53
  71.9 3.1 %fusion.14 = f32[1024,768]{1,0:T(8,128)} fusion(f32[256,768]{1,0:T(8,128)S(1)} %bitcast.61, f32[128,8,2,128]{3,2,1,0:T(2,128)S(1)} %bitcast.59), kind=kOutput, calls=%fused_computation.16 | convolution fusion | flops 1207959552 | bytes 4980736 | tf_op jit(solution)/shard_map/dot_general | solution.py:18
  75.0 0.0 all-reduce.3.cloned.1.call-update
  75.0 0.2 all-reduce.5.cloned.1.call-start
  75.3 0.3 copy.24
  75.5 0.0 all-gather.4.cloned.1.call-done
  75.6 85.3 %all-reduce.3.cloned.1.call-done = f32[1024,768]{1,0:T(8,128)} async-done(((f32[1024,768]{1,0:T(8,128)}), f32[1024,768]{1,0:T(8,128)}) %all-reduce.3.cloned.1.call-update) | async-done | bytes 3145744 | tf_op jit(solution)/shard_map/psum | solution.py:48
  160.9 4.8 %fusion.8 = f32[256,768]{0,1:T(8,128)S(1)} fusion(f32[256,768]{0,1:T(8,128)S(1)} %copy.24, f32[1024,768]{1,0:T(8,128)} %all-reduce.3.cloned.1.call-done, f32[128,8,2,128]{3,2,1,0:T(2,128)} %bitcast.66), kind=kOutput, calls=%fused_computation.10 | convolution fusion | flops 1208156160 | bytes 5767168 | tf_op jit(solution)/shard_map/dot_general | solution.py:22
  165.7 0.0 copy-start.4
  165.7 3.1 %fusion.11 = f32[1024,768]{1,0:T(8,128)} fusion(f32[256,768]{0,1:T(8,128)S(1)} %fusion.8, f32[128,8,2,128]{3,2,1,0:T(2,128)S(1)} %bitcast.58), kind=kOutput, calls=%fused_computation.13 | convolution fusion | flops 1207959552 | bytes 4980736 | tf_op jit(solution)/shard_map/dot_general | solution.py:18
  168.8 0.0 all-reduce.5.cloned.1.call-update
  168.9 0.0 all-gather.8.cloned.1.call-start
  168.9 0.7 all-gather.8.cloned.1.call-update
  169.6 0.0 all-gather.6.cloned.1.call-start
  169.7 0.0 copy-done.4
  169.7 0.8 slice.41
  170.5 0.0 all-gather.6.cloned.1.call-update
  170.5 3.8 %slice.39 = f32[8,1,128,768]{3,2,1,0:T(8,128)} slice(f32[12,1,128,768]{3,2,1,0:T(8,128)} %param.4), slice={[4:12], [0:1], [0:128], [0:768]} | slice | bytes 6291456 | tf_op jit(solution)/shard_map/slice | solution.py:63
  174.3 4.1 %copy.26 = f32[1024,768]{0,1:T(8,128)} copy(f32[1024,768]{1,0:T(8,128)} %bitcast.57) | data formatting | bytes 6291456 | tf_op jit(solution)/shard_map/slice | solution.py:63
  178.4 1.0 constant_dynamic-slice_fusion.1
  179.4 2.4 copy.23
  181.8 73.9 %all-reduce.5.cloned.1.call-done = f32[1024,768]{1,0:T(8,128)} async-done(((f32[1024,768]{1,0:T(8,128)}), f32[1024,768]{1,0:T(8,128)}) %all-reduce.5.cloned.1.call-update) | async-done | bytes 3145744 | tf_op jit(solution)/shard_map/psum | solution.py:52
  255.6 2.1 constant_dynamic-slice_fusion
  257.7 2.3 copy.25
  260.0 9.7 %fusion = f32[768,1024]{1,0:T(8,128)} fusion(f32[1024,768]{1,0:T(8,128)} %all-reduce.5.cloned.1.call-done, f32[128,8,8,128]{3,2,1,0:T(8,128)} %bitcast.70), kind=kOutput, calls=%fused_computation.1 | convolution fusion | flops 4831838208 | bytes 10485760 | tf_op jit(solution)/shard_map/dot_general | solution.py:22
  269.7 9.4 %bitcast_subtract_fusion = f32[1024,768]{0,1:T(8,128)S(1)} fusion(f32[768,1024]{1,0:T(8,128)} %fusion, f32[1024,768]{0,1:T(8,128)} %copy.26, f32[1024,768]{1,0:T(8,128)S(1)} %copy-done, f32[128,8,8,128]{3,2,1,0:T(8,128)} %bitcast.60), kind=kOutput, calls=%fused_computation.7 | convolution fusion | flops 4833411072 | bytes 16777216 | tf_op jit(solution)/shard_map/dot_general | solution.py:22
  279.2 2.6 pad_maximum_fusion
  281.8 6.0 %copy.21 = f32[1536,768]{1,0:T(8,128)} copy(f32[1536,768]{0,1:T(8,128)} %pad_maximum_fusion) | data formatting | bytes 9437184 | tf_op jit(solution)/shard_map/concatenate | solution.py:67
  (9 shorter events, 0.0 us)
Async XLA Ops:
  7.4 56.0 %copy-start.3 = (f32[2,128,2,1,128]{4,3,2,1,0:T(1,128)S(1)}, f32[2,128,2,1,128]{4,3,2,1,0:T(1,128)}, u32[]{:S(2)}) copy-start(f32[2,128,2,1,128]{4,3,2,1,0:T(1,128)} %param.7) | copy-start | bytes 786436
  7.4 68.2 %all-gather.4.cloned.1.call-start = ((), (), s32[]{:S(2)}) async-start(), calls=%async_computation.1 | async-start | bytes 1179648 | tf_op jit(solution)/shard_map/all_gather | solution.py:49
  7.4 8.8 %collective-permute-start = (f32[2,128,2,1,128]{4,3,2,1,0:T(1,128)}, f32[2,128,2,1,128]{4,3,2,1,0:T(1,128)S(1)}, u32[]{:S(2)}, u32[]{:S(2)}) collective-permute-start(f32[2,128,2,1,128]{4,3,2,1,0:T(1,128)} %param.7), channel_id=1, source_target_pairs={{0,1},{1,2},{2,3},{3,4},{4,5},{5,6},{6,7},{7,0},{8,9},{9,10},{10,1... | collective-permute-start | bytes 786440 | tf_op jit(solution)/shard_map/ppermute | solution.py:11
  16.2 7.6 %collective-permute-start.1 = (f32[2,128,2,1,128]{4,3,2,1,0:T(1,128)S(1)}, f32[2,128,2,1,128]{4,3,2,1,0:T(1,128)S(1)}, u32[]{:S(2)}, u32[]{:S(2)}) collective-permute-start(f32[2,128,2,1,128]{4,3,2,1,0:T(1,128)S(1)} %collective-permute-done), channel_id=1, source_target_pairs={{0,1},{1,2},{2,3},{3,4},{4,5},{5,6},{6,7},{7,0},{8,9},{9,10},{10,1... | collective-permute-start | bytes 786440 | tf_op jit(solution)/shard_map/ppermute | solution.py:11
  23.8 7.6 %collective-permute-start.2 = (f32[2,128,2,1,128]{4,3,2,1,0:T(1,128)S(1)}, f32[2,128,2,1,128]{4,3,2,1,0:T(1,128)S(1)}, u32[]{:S(2)}, u32[]{:S(2)}) collective-permute-start(f32[2,128,2,1,128]{4,3,2,1,0:T(1,128)S(1)} %collective-permute-done.1), channel_id=1, source_target_pairs={{0,1},{1,2},{2,3},{3,4},{4,5},{5,6},{6,7},{7,0},{8,9},{9,10},{10,1... | collective-permute-start | bytes 786440 | tf_op jit(solution)/shard_map/ppermute | solution.py:11
  31.4 7.6 %collective-permute-start.3 = (f32[2,128,2,1,128]{4,3,2,1,0:T(1,128)S(1)}, f32[2,128,2,1,128]{4,3,2,1,0:T(1,128)S(1)}, u32[]{:S(2)}, u32[]{:S(2)}) collective-permute-start(f32[2,128,2,1,128]{4,3,2,1,0:T(1,128)S(1)} %collective-permute-done.2), channel_id=1, source_target_pairs={{0,1},{1,2},{2,3},{3,4},{4,5},{5,6},{6,7},{7,0},{8,9},{9,10},{10,1... | collective-permute-start | bytes 786440 | tf_op jit(solution)/shard_map/ppermute | solution.py:11
  39.0 7.6 %collective-permute-start.4 = (f32[2,128,2,1,128]{4,3,2,1,0:T(1,128)S(1)}, f32[2,128,2,1,128]{4,3,2,1,0:T(1,128)S(1)}, u32[]{:S(2)}, u32[]{:S(2)}) collective-permute-start(f32[2,128,2,1,128]{4,3,2,1,0:T(1,128)S(1)} %collective-permute-done.3), channel_id=1, source_target_pairs={{0,1},{1,2},{2,3},{3,4},{4,5},{5,6},{6,7},{7,0},{8,9},{9,10},{10,1... | collective-permute-start | bytes 786440 | tf_op jit(solution)/shard_map/ppermute | solution.py:11
  46.6 7.6 %collective-permute-start.5 = (f32[2,128,2,1,128]{4,3,2,1,0:T(1,128)S(1)}, f32[2,128,2,1,128]{4,3,2,1,0:T(1,128)S(1)}, u32[]{:S(2)}, u32[]{:S(2)}) collective-permute-start(f32[2,128,2,1,128]{4,3,2,1,0:T(1,128)S(1)} %collective-permute-done.4), channel_id=1, source_target_pairs={{0,1},{1,2},{2,3},{3,4},{4,5},{5,6},{6,7},{7,0},{8,9},{9,10},{10,1... | collective-permute-start | bytes 786440 | tf_op jit(solution)/shard_map/ppermute | solution.py:11
  48.2 112.7 %all-reduce.3.cloned.1.call-start = ((), (), s32[]{:S(2)}) async-start(), calls=%async_computation | async-start | bytes 6291456 | tf_op jit(solution)/shard_map/psum | solution.py:48
  54.2 7.8 %collective-permute-start.6 = (f32[2,128,2,1,128]{4,3,2,1,0:T(1,128)S(1)}, f32[2,128,2,1,128]{4,3,2,1,0:T(1,128)S(1)}, u32[]{:S(2)}, u32[]{:S(2)}) collective-permute-start(f32[2,128,2,1,128]{4,3,2,1,0:T(1,128)S(1)} %collective-permute-done.5), channel_id=1, source_target_pairs={{0,1},{1,2},{2,3},{3,4},{4,5},{5,6},{6,7},{7,0},{8,9},{9,10},{10,1... | collective-permute-start | bytes 786440 | tf_op jit(solution)/shard_map/ppermute | solution.py:11
  75.0 180.6 %all-reduce.5.cloned.1.call-start = ((), (), s32[]{:S(2)}) async-start(), calls=%async_computation.2 | async-start | bytes 6291456 | tf_op jit(solution)/shard_map/psum | solution.py:52
  165.7 4.0 %copy-start.4 = (f32[128,10,1,128]{3,2,1,0:T(1,128)S(1)}, f32[128,10,1,128]{3,2,1,0:T(1,128)}, u32[]{:S(2)}) copy-start(f32[128,10,1,128]{3,2,1,0:T(1,128)} %param.5) | copy-start | bytes 1966084
  168.9 91.1 %all-gather.8.cloned.1.call-start = ((), (), s32[]{:S(2)}) async-start(), calls=%async_computation.4 | async-start | bytes 4718592 | tf_op jit(solution)/shard_map/all_gather | solution.py:57
  169.6 100.1 %all-gather.6.cloned.1.call-start = ((), (), s32[]{:S(2)}) async-start(), calls=%async_computation.3 | async-start | bytes 4718592 | tf_op jit(solution)/shard_map/all_gather | solution.py:56
  174.3 4.1 %copy-start = (f32[1024,768]{1,0:T(8,128)S(1)}, f32[1024,768]{1,0:T(8,128)}, u32[]{:S(2)}) copy-start(f32[1024,768]{1,0:T(8,128)} %all-reduce.3.cloned.1.call-done) | copy-start | bytes 9437188
  269.7 9.4 %copy-start.1 = (f32[256,768]{0,1:T(8,128)S(1)}, f32[256,768]{0,1:T(8,128)}, u32[]{:S(2)}) copy-start(f32[256,768]{0,1:T(8,128)} %copy.23) | copy-start | bytes 2359300
  269.7 9.4 %copy-start.2 = (f32[256,768]{0,1:T(8,128)S(1)}, f32[256,768]{0,1:T(8,128)}, u32[]{:S(2)}) copy-start(f32[256,768]{0,1:T(8,128)} %copy.25) | copy-start | bytes 2359300
Sparse Core Ops, SparseCore 0:
  48.3 24.7 all-gather.3
  171.3 46.8 all-gather.7
  219.8 45.6 all-gather.5
Sparse Core Ops, SparseCore 1:
  75.1 85.7 all-reduce.2
  168.9 86.6 all-reduce.4
